TPU v7x, 256 devices: a whole 4x4x8 slice. The times are simulated.
256 devices in a mesh: seq: 64 (over z, y, core), tp: 4 (over x).
Axes of the slice: x: 4, y: 4, z: 8, core: 2. Of those that a mesh axis runs over, the one named last changes fastest.
Arguments:
- tokens: bfloat16 [8192, 3584], P('seq', 'tp'), may hold values from -24 to 24
- modality: int32 [64], P('seq'), may hold values from 0 to 1
- segment: int32 [8192], P('seq'), may hold values from 0 to 3, never falling along the last dimension, each value on 1 to 4096 neighbouring positions
- w_proj: bfloat16 [2, 3584, 4608], P(None, 'seq', 'tp'), may hold values from -1 to 1
Outputs:
- attended: bfloat16 [8192, 3584], P('seq', 'tp')
Inputs may be any that keep to these rules, and one draw needn't show every extreme that they name: `modality`: 128 consecutive tokens share one label: 0 marks an understanding block, 1 a generation block. `segment`: sample numbers never fall along the tokens.
All inputs are finite; a program needn't handle non-finite values.
Results may differ from a plain program's by a relative error of at most 0.0086.
Values may be sent and summed in bfloat16 or wider, within the bound.
A program may use at most 128 MiB of HBM per device.

v0:
```python
import math

import jax
import jax.numpy as jnp
from jax import lax
from jax.sharding import PartitionSpec as P

QUERY_HEADS = 28
KEY_VALUE_HEADS = 4
HEAD_SIZE = 128
MODALITY_BLOCK = 128


masked_score = -1e30


def laid_out(blocks, dim):
    dims = list(blocks.shape[1:])
    dims[dim] *= blocks.shape[0]
    return jnp.moveaxis(blocks, 0, dim).reshape(dims)


def copy_for_each(array, axis):
    peers = lax.axis_size(axis)
    return lax.all_to_all(
        jnp.broadcast_to(array[None], (peers, *array.shape)), axis, 0, 0, tiled=True
    )


def collect(array, axis, dim):
    return laid_out(copy_for_each(array, axis), dim)


def sent_together(arrays, axis, dim, along):
    ends, at = ([], 0)
    for a in arrays[:-1]:
        at += a.shape[along]
        ends.append(at)
    both = jnp.concatenate(arrays, axis=along)
    return tuple(jnp.split(lax.all_gather(both, axis, axis=dim, tiled=True), ends, axis=along))


def local(tokens, modality, segment, w_proj):
    rows_here = tokens.shape[0]
    group_width = QUERY_HEADS // KEY_VALUE_HEADS
    width_here = w_proj.shape[2]
    gathered = collect(tokens, "tp", 1)
    shard_piece = lax.all_gather(w_proj, "seq", axis=1, tiled=True)
    chosen = jnp.where(modality[0] == 1, shard_piece[1], shard_piece[0])
    results = jnp.dot(gathered, chosen, preferred_element_type=jnp.float32)
    projected_tokens = results
    projected_tokens = projected_tokens.astype(jnp.bfloat16)
    head_groups = width_here // ((group_width + 2) * HEAD_SIZE)
    shaped = projected_tokens.reshape(rows_here, head_groups, group_width + 2, HEAD_SIZE)
    queries = shaped[:, :, :group_width]
    key_rows = shaped[:, :, group_width]
    values = shaped[:, :, group_width + 1]
    seq_index = lax.axis_index("seq")
    row_numbers = jnp.arange(rows_here, dtype=jnp.int32)
    row_labels = jnp.repeat(modality, MODALITY_BLOCK)
    query_pos = seq_index * rows_here + row_numbers
    query_block = query_pos // MODALITY_BLOCK
    query_gen = row_labels == 1
    reach = jnp.where(query_gen, (query_block + 1) * MODALITY_BLOCK - 1, query_pos)
    reach_limit = jnp.max(reach)
    query_lay = jnp.transpose(queries, (1, 2, 0, 3)).reshape(
        head_groups, group_width * rows_here, HEAD_SIZE
    )
    tiled_pos = jnp.tile(query_pos, group_width)
    tiled_seg = jnp.tile(segment, group_width)
    tiled_block = jnp.tile(query_block, group_width)
    tiled_gen = jnp.tile(query_gen, group_width)
    inverse_root = 1.0 / math.sqrt(HEAD_SIZE)

    def absorb(carried, key_part, value_part, key_seg, offset):
        key_pos = offset + jnp.arange(key_part.shape[0], dtype=jnp.int32)
        allowed = (tiled_seg[:, None] == key_seg[None, :]) & (
            (key_pos[None, :] <= tiled_pos[:, None])
            | (key_pos[None, :] // MODALITY_BLOCK == tiled_block[:, None]) & tiled_gen[:, None]
        )
        scores = (
            jnp.einsum("gqd,kgd->gqk", query_lay, key_part, preferred_element_type=jnp.float32)
            * inverse_root
        )
        scores = jnp.where(allowed[None], scores, masked_score)
        running_max, running_sum, running_acc = carried
        new_max = jnp.maximum(running_max, jnp.max(scores, axis=2))
        weights = jnp.where(allowed[None], jnp.exp(scores - new_max[:, :, None]), 0.0)
        shrink = jnp.exp(running_max - new_max)
        running_sum = running_sum * shrink + jnp.sum(weights, axis=2)
        running_acc = running_acc * shrink[:, :, None] + jnp.einsum(
            "gqk,kgd->gqd",
            weights.astype(jnp.bfloat16),
            value_part,
            preferred_element_type=jnp.float32,
        )
        return (new_max, running_sum, running_acc)

    query_total = group_width * rows_here
    initial = (
        jnp.full((head_groups, query_total), masked_score, jnp.float32),
        jnp.zeros((head_groups, query_total), jnp.float32),
        jnp.zeros((head_groups, query_total, HEAD_SIZE), jnp.float32),
    )
    key_part, value_part, key_seg = (
        *sent_together((key_rows, values), "seq", 0, 1),
        lax.all_gather(segment, "seq", axis=0, tiled=True),
    )
    length = key_part.shape[0]
    key_span = 1024

    def compute(state_in):
        key_steps = length // key_span

        def absorb_block(state_now, scan_item):
            part_keys, part_values, part_seg, part_offset = scan_item
            return (absorb(state_now, part_keys, part_values, part_seg, part_offset), None)

        offsets = jnp.arange(key_steps, dtype=jnp.int32) * key_span
        state_out, unused = lax.scan(
            absorb_block,
            state_in,
            (
                key_part.reshape((key_steps, key_span) + key_part.shape[1:]),
                value_part.reshape((key_steps, key_span) + value_part.shape[1:]),
                key_seg.reshape(key_steps, key_span),
                offsets,
            ),
        )
        return state_out

    def passing(state_in):
        return state_in

    final_max, final_sum, final_acc = lax.cond(
        jnp.int32(0) <= reach_limit, compute, passing, initial
    )
    answer = (final_acc / final_sum[:, :, None]).astype(jnp.bfloat16)
    answer = jnp.transpose(
        answer.reshape(head_groups, group_width, rows_here, HEAD_SIZE), (2, 0, 1, 3)
    )
    return answer.reshape(rows_here, head_groups * group_width * HEAD_SIZE)


def solution(mesh):
    return jax.shard_map(
        local,
        mesh=mesh,
        in_specs=(P("seq", "tp"), P("seq"), P("seq"), P(None, "seq", "tp")),
        out_specs=P("seq", "tp"),
        check_vma=False,
    )
```

profile of v0, /device:TPU:1, one launch (start us, length us, event | category | flops | bytes accessed | tf_op | source)
XLA Modules:
  0.0 331.3 jit_solution(6506443907413860339)
XLA Ops:
  6.5 0.7 all-gather.4.cloned.1.call-update
  7.3 1.1 copy.26
  8.4 1.1 broadcast_in_dim.40
  9.4 4.8 %all-to-all-start = ((bf16[4,128,896]{1,2,0:T(8,128)(2,1)}), bf16[4,128,896]{1,2,0:T(8,128)(2,1)S(1)}, u32[]{:S(2)}, u32[]{:S(2)}) async-start(bf16[4,128,896]{1,2,0:T(8,128)(2,1)} %broadcast_in_dim.40), calls=%async_computation | async-start | bytes 1835008 | tf_op jit(solution)/shard_map/all_to_all | solution.py:25
  14.9 11.3 %all-to-all-done = bf16[4,128,896]{1,2,0:T(8,128)(2,1)S(1)} async-done(((bf16[4,128,896]{1,2,0:T(8,128)(2,1)}), bf16[4,128,896]{1,2,0:T(8,128)(2,1)S(1)}, u32[]{:S(2)}, u32[]{:S(2)}) %all-to-all-start) | async-done | bytes 917536 | tf_op jit(solution)/shard_map/all_to_all | solution.py:25
  26.2 86.6 %all-gather.4.cloned.1.call-done = bf16[2,3584,1152]{2,1,0:T(8,128)(2,1)} async-done(((bf16[2,56,1152]{2,1,0:T(8,128)(2,1)}), bf16[2,3584,1152]{2,1,0:T(8,128)(2,1)}) %all-gather.4.cloned.1.call-update) | async-done | bytes 16515088 | tf_op jit(solution)/shard_map/all_gather | solution.py:48
  112.8 8.2 %fusion.42 = bf16[1152,128]{1,0:T(8,128)(2,1)S(1)} fusion(bf16[128,3584]{0,1:T(8,128)(2,1)S(1)} %bitcast.97, bf16[2,3584,1152]{2,1,0:T(8,128)(2,1)} %all-gather.4.cloned.1.call-done, pred[]{:T(512)} %bitcast), kind=kOutput, calls=%fused_computation.57 | convolution fusion | flops 1061240832 | bytes 17727488 | tf_op jit(solution)/shard_map/dot_general | solution.py:50
  121.3 0.6 pad_maximum_fusion
  121.9 0.6 fusion.45
  123.2 38.5 %all-gather = s32[64,1,128]{2,1,0:T(1,128)S(1)} all-gather(s32[1,1,128]{2,1,0:T(1,128)S(1)} %bitcast.110), channel_id=1, replica_groups=mesh['seq'=64,'tp'=4] {'seq'}, dimensions={0}, use_global_device_ids=true | all-gather | bytes 33280 | tf_op jit(solution)/shard_map/all_gather | solution.py:107
  161.8 36.3 %all-gather.6.cloned.1.call-done = bf16[8192,2,128]{2,0,1:T(8,128)(2,1)} async-done(((bf16[128,2,128]{2,0,1:T(8,128)(2,1)}), bf16[8192,2,128]{2,0,1:T(8,128)(2,1)}) %all-gather.6.cloned.1.call-update) | async-done | bytes 4194320 | tf_op jit(solution)/shard_map/all_gather | solution.py:40
  198.2 123.4 %conditional.1 = (f32[1,896]{1,0:T(1,128)}, f32[1,896,128]{2,1,0:T(8,128)}) conditional(s32[]{:T(128)} %convert_element_type.19, () %tuple.28, (bf16[8192,2,128]{2,0,1:T(8,128)(2,1)}, s32[8192]{0:T(1024)S(1)}, s32[128]{0:T(128)S(1)}, s32[]{:T(128)}, s32[1,128]{1,0:T(1,128)S(1)}, /*index=5*/s32[]{:T(128)}, pred[]{:T(512)}, ...), branch_computations={%region_1.2_spmd, %region_2.7_spmd.clone} | conditional | flops 498572544 | bytes 35979656 | solution.py:135
  198.2 3.9 %fusion.46 = (bf16[8192,1,128]{2,0,1:T(8,128)(2,1)S(1)}, bf16[8192,1,128]{2,0,1:T(8,128)(2,1)}) fusion(bf16[8192,2,128]{2,0,1:T(8,128)(2,1)} %get-tuple-element.279), kind=kLoop, calls=%fused_computation.66 | loop fusion | bytes 8388608 | tf_op jit(solution)/shard_map/split | solution.py:40
  202.1 119.4 %while.20 = (s32[]{:T(128)}, f32[1,896]{1,0:T(1,128)S(1)}, f32[1,896]{1,0:T(1,128)}, f32[1,896,128]{2,1,0:T(8,128)}, s32[8,1024]{1,0:T(8,128)S(1)}, /*index=5*/s...) while((s32[]{:T(128)}, f32[1,896]{1,0:T(1,128)S(1)}, ...), condition=%wide.region_6.6_spmd.clone, body=%wide.region_3.5_spmd.clone.sunk | while | flops 498570496 | bytes 27523792 | solution.py:120
  202.1 0.6 dynamic_slice.49
  202.7 0.6 add_select_fusion.2
  203.3 4.4 %fusion.58 = (f32[896]{0:T(1024)S(1)}, f32[1024,896]{1,0:T(8,128)}) fusion(pred[]{:T(512)} %get-tuple-element.569, s32[896]{0:T(1024)S(1)} %get-tuple-element.518, s32[1024]{0:T(1024)S(1)} %get-tuple-element.519, s32[896]{0:T(1024)S(1)} %get-tuple-element.520, s32[1024]{0:T(1024)S(1)} %get-tuple-element.521, s32[1024]{0:T(1024)S(1)} %bitcast.100, ...), kind=kOutput, calls=%fused_computation.7.clone.1 | convolution fusion | flops 243137664 | bytes 4189184 | tf_op jit(solution)/shard_map/cond/branch_1_fun/while/body/eval_jaxpr/gqd,kgd->gqk/dot_general | solution.py:82
  207.8 5.5 %fusion.62 = f32[1,896,128]{2,1,0:T(8,128)} fusion(f32[1024,896]{1,0:T(8,128)} %get-tuple-element.524, f32[896]{0:T(1024)S(1)} %get-tuple-element.525, f32[1,896,128]{2,1,0:T(8,128)} %get-tuple-element.545, bf16[8,1024,1,128]{3,1,2,0:T(8,128)(2,1)S(1)} %get-tuple-element.565, s32[]{:T(128)} %get-tuple-element.542, f32[896]{0:T(1024)S(1)} %get-tuple-element.526, ...), kind=kOutput, calls=%fused_computation.12.clone.1 | convolution fusion | flops 245317632 | bytes 4882438 | tf_op jit(solution)/shard_map/cond/branch_1_fun/while/body/eval_jaxpr/gqk,kgd->gqd/dot_general | solution.py:91
  213.3 2.5 fusion.60
  215.8 0.6 fusion.61
  216.4 0.6 dynamic_slice.49
  217.0 0.6 add_select_fusion.2
  217.6 4.4 %fusion.58 = (f32[896]{0:T(1024)S(1)}, f32[1024,896]{1,0:T(8,128)}) fusion(pred[]{:T(512)} %get-tuple-element.569, s32[896]{0:T(1024)S(1)} %get-tuple-element.518, s32[1024]{0:T(1024)S(1)} %get-tuple-element.519, s32[896]{0:T(1024)S(1)} %get-tuple-element.520, s32[1024]{0:T(1024)S(1)} %get-tuple-element.521, s32[1024]{0:T(1024)S(1)} %bitcast.100, ...), kind=kOutput, calls=%fused_computation.7.clone.1 | convolution fusion | flops 243137664 | bytes 4189184 | tf_op jit(solution)/shard_map/cond/branch_1_fun/while/body/eval_jaxpr/gqd,kgd->gqk/dot_general | solution.py:82
  222.1 5.6 %fusion.62 = f32[1,896,128]{2,1,0:T(8,128)} fusion(f32[1024,896]{1,0:T(8,128)} %get-tuple-element.524, f32[896]{0:T(1024)S(1)} %get-tuple-element.525, f32[1,896,128]{2,1,0:T(8,128)} %get-tuple-element.545, bf16[8,1024,1,128]{3,1,2,0:T(8,128)(2,1)S(1)} %get-tuple-element.565, s32[]{:T(128)} %get-tuple-element.542, f32[896]{0:T(1024)S(1)} %get-tuple-element.526, ...), kind=kOutput, calls=%fused_computation.12.clone.1 | convolution fusion | flops 245317632 | bytes 4882438 | tf_op jit(solution)/shard_map/cond/branch_1_fun/while/body/eval_jaxpr/gqk,kgd->gqd/dot_general | solution.py:91
  227.6 2.5 fusion.60
  230.1 1.3 fusion.61
  231.4 0.6 dynamic_slice.49
  232.0 0.6 add_select_fusion.2
  232.6 4.4 %fusion.58 = (f32[896]{0:T(1024)S(1)}, f32[1024,896]{1,0:T(8,128)}) fusion(pred[]{:T(512)} %get-tuple-element.569, s32[896]{0:T(1024)S(1)} %get-tuple-element.518, s32[1024]{0:T(1024)S(1)} %get-tuple-element.519, s32[896]{0:T(1024)S(1)} %get-tuple-element.520, s32[1024]{0:T(1024)S(1)} %get-tuple-element.521, s32[1024]{0:T(1024)S(1)} %bitcast.100, ...), kind=kOutput, calls=%fused_computation.7.clone.1 | convolution fusion | flops 243137664 | bytes 4189184 | tf_op jit(solution)/shard_map/cond/branch_1_fun/while/body/eval_jaxpr/gqd,kgd->gqk/dot_general | solution.py:82
  237.1 5.6 %fusion.62 = f32[1,896,128]{2,1,0:T(8,128)} fusion(f32[1024,896]{1,0:T(8,128)} %get-tuple-element.524, f32[896]{0:T(1024)S(1)} %get-tuple-element.525, f32[1,896,128]{2,1,0:T(8,128)} %get-tuple-element.545, bf16[8,1024,1,128]{3,1,2,0:T(8,128)(2,1)S(1)} %get-tuple-element.565, s32[]{:T(128)} %get-tuple-element.542, f32[896]{0:T(1024)S(1)} %get-tuple-element.526, ...), kind=kOutput, calls=%fused_computation.12.clone.1 | convolution fusion | flops 245317632 | bytes 4882438 | tf_op jit(solution)/shard_map/cond/branch_1_fun/while/body/eval_jaxpr/gqk,kgd->gqd/dot_general | solution.py:91
  242.7 2.5 fusion.60
  245.1 1.3 fusion.61
  246.4 0.6 dynamic_slice.49
  247.0 0.6 add_select_fusion.2
  247.6 4.4 %fusion.58 = (f32[896]{0:T(1024)S(1)}, f32[1024,896]{1,0:T(8,128)}) fusion(pred[]{:T(512)} %get-tuple-element.569, s32[896]{0:T(1024)S(1)} %get-tuple-element.518, s32[1024]{0:T(1024)S(1)} %get-tuple-element.519, s32[896]{0:T(1024)S(1)} %get-tuple-element.520, s32[1024]{0:T(1024)S(1)} %get-tuple-element.521, s32[1024]{0:T(1024)S(1)} %bitcast.100, ...), kind=kOutput, calls=%fused_computation.7.clone.1 | convolution fusion | flops 243137664 | bytes 4189184 | tf_op jit(solution)/shard_map/cond/branch_1_fun/while/body/eval_jaxpr/gqd,kgd->gqk/dot_general | solution.py:82
  252.1 5.6 %fusion.62 = f32[1,896,128]{2,1,0:T(8,128)} fusion(f32[1024,896]{1,0:T(8,128)} %get-tuple-element.524, f32[896]{0:T(1024)S(1)} %get-tuple-element.525, f32[1,896,128]{2,1,0:T(8,128)} %get-tuple-element.545, bf16[8,1024,1,128]{3,1,2,0:T(8,128)(2,1)S(1)} %get-tuple-element.565, s32[]{:T(128)} %get-tuple-element.542, f32[896]{0:T(1024)S(1)} %get-tuple-element.526, ...), kind=kOutput, calls=%fused_computation.12.clone.1 | convolution fusion | flops 245317632 | bytes 4882438 | tf_op jit(solution)/shard_map/cond/branch_1_fun/while/body/eval_jaxpr/gqk,kgd->gqd/dot_general | solution.py:91
  257.7 2.5 fusion.60
  260.2 1.3 fusion.61
  261.5 0.6 dynamic_slice.49
  262.0 0.6 add_select_fusion.2
  262.6 4.4 %fusion.58 = (f32[896]{0:T(1024)S(1)}, f32[1024,896]{1,0:T(8,128)}) fusion(pred[]{:T(512)} %get-tuple-element.569, s32[896]{0:T(1024)S(1)} %get-tuple-element.518, s32[1024]{0:T(1024)S(1)} %get-tuple-element.519, s32[896]{0:T(1024)S(1)} %get-tuple-element.520, s32[1024]{0:T(1024)S(1)} %get-tuple-element.521, s32[1024]{0:T(1024)S(1)} %bitcast.100, ...), kind=kOutput, calls=%fused_computation.7.clone.1 | convolution fusion | flops 243137664 | bytes 4189184 | tf_op jit(solution)/shard_map/cond/branch_1_fun/while/body/eval_jaxpr/gqd,kgd->gqk/dot_general | solution.py:82
  267.1 5.6 %fusion.62 = f32[1,896,128]{2,1,0:T(8,128)} fusion(f32[1024,896]{1,0:T(8,128)} %get-tuple-element.524, f32[896]{0:T(1024)S(1)} %get-tuple-element.525, f32[1,896,128]{2,1,0:T(8,128)} %get-tuple-element.545, bf16[8,1024,1,128]{3,1,2,0:T(8,128)(2,1)S(1)} %get-tuple-element.565, s32[]{:T(128)} %get-tuple-element.542, f32[896]{0:T(1024)S(1)} %get-tuple-element.526, ...), kind=kOutput, calls=%fused_computation.12.clone.1 | convolution fusion | flops 245317632 | bytes 4882438 | tf_op jit(solution)/shard_map/cond/branch_1_fun/while/body/eval_jaxpr/gqk,kgd->gqd/dot_general | solution.py:91
  272.7 2.5 fusion.60
  275.2 1.3 fusion.61
  276.5 0.6 dynamic_slice.49
  277.0 0.6 add_select_fusion.2
  277.7 4.4 %fusion.58 = (f32[896]{0:T(1024)S(1)}, f32[1024,896]{1,0:T(8,128)}) fusion(pred[]{:T(512)} %get-tuple-element.569, s32[896]{0:T(1024)S(1)} %get-tuple-element.518, s32[1024]{0:T(1024)S(1)} %get-tuple-element.519, s32[896]{0:T(1024)S(1)} %get-tuple-element.520, s32[1024]{0:T(1024)S(1)} %get-tuple-element.521, s32[1024]{0:T(1024)S(1)} %bitcast.100, ...), kind=kOutput, calls=%fused_computation.7.clone.1 | convolution fusion | flops 243137664 | bytes 4189184 | tf_op jit(solution)/shard_map/cond/branch_1_fun/while/body/eval_jaxpr/gqd,kgd->gqk/dot_general | solution.py:82
  282.1 5.6 %fusion.62 = f32[1,896,128]{2,1,0:T(8,128)} fusion(f32[1024,896]{1,0:T(8,128)} %get-tuple-element.524, f32[896]{0:T(1024)S(1)} %get-tuple-element.525, f32[1,896,128]{2,1,0:T(8,128)} %get-tuple-element.545, bf16[8,1024,1,128]{3,1,2,0:T(8,128)(2,1)S(1)} %get-tuple-element.565, s32[]{:T(128)} %get-tuple-element.542, f32[896]{0:T(1024)S(1)} %get-tuple-element.526, ...), kind=kOutput, calls=%fused_computation.12.clone.1 | convolution fusion | flops 245317632 | bytes 4882438 | tf_op jit(solution)/shard_map/cond/branch_1_fun/while/body/eval_jaxpr/gqk,kgd->gqd/dot_general | solution.py:91
  287.7 2.5 fusion.60
  290.2 1.3 fusion.61
  292.1 0.6 add_select_fusion.2
  292.7 4.4 %fusion.58 = (f32[896]{0:T(1024)S(1)}, f32[1024,896]{1,0:T(8,128)}) fusion(pred[]{:T(512)} %get-tuple-element.569, s32[896]{0:T(1024)S(1)} %get-tuple-element.518, s32[1024]{0:T(1024)S(1)} %get-tuple-element.519, s32[896]{0:T(1024)S(1)} %get-tuple-element.520, s32[1024]{0:T(1024)S(1)} %get-tuple-element.521, s32[1024]{0:T(1024)S(1)} %bitcast.100, ...), kind=kOutput, calls=%fused_computation.7.clone.1 | convolution fusion | flops 243137664 | bytes 4189184 | tf_op jit(solution)/shard_map/cond/branch_1_fun/while/body/eval_jaxpr/gqd,kgd->gqk/dot_general | solution.py:82
  297.2 5.6 %fusion.62 = f32[1,896,128]{2,1,0:T(8,128)} fusion(f32[1024,896]{1,0:T(8,128)} %get-tuple-element.524, f32[896]{0:T(1024)S(1)} %get-tuple-element.525, f32[1,896,128]{2,1,0:T(8,128)} %get-tuple-element.545, bf16[8,1024,1,128]{3,1,2,0:T(8,128)(2,1)S(1)} %get-tuple-element.565, s32[]{:T(128)} %get-tuple-element.542, f32[896]{0:T(1024)S(1)} %get-tuple-element.526, ...), kind=kOutput, calls=%fused_computation.12.clone.1 | convolution fusion | flops 245317632 | bytes 4882438 | tf_op jit(solution)/shard_map/cond/branch_1_fun/while/body/eval_jaxpr/gqk,kgd->gqd/dot_general | solution.py:91
  302.7 2.5 fusion.60
  305.2 1.3 fusion.61
  306.5 0.6 dynamic_slice.49
  307.1 0.6 add_select_fusion.2
  307.7 4.4 %fusion.58 = (f32[896]{0:T(1024)S(1)}, f32[1024,896]{1,0:T(8,128)}) fusion(pred[]{:T(512)} %get-tuple-element.569, s32[896]{0:T(1024)S(1)} %get-tuple-element.518, s32[1024]{0:T(1024)S(1)} %get-tuple-element.519, s32[896]{0:T(1024)S(1)} %get-tuple-element.520, s32[1024]{0:T(1024)S(1)} %get-tuple-element.521, s32[1024]{0:T(1024)S(1)} %bitcast.100, ...), kind=kOutput, calls=%fused_computation.7.clone.1 | convolution fusion | flops 243137664 | bytes 4189184 | tf_op jit(solution)/shard_map/cond/branch_1_fun/while/body/eval_jaxpr/gqd,kgd->gqk/dot_general | solution.py:82
  312.2 5.6 %fusion.62 = f32[1,896,128]{2,1,0:T(8,128)} fusion(f32[1024,896]{1,0:T(8,128)} %get-tuple-element.524, f32[896]{0:T(1024)S(1)} %get-tuple-element.525, f32[1,896,128]{2,1,0:T(8,128)} %get-tuple-element.545, bf16[8,1024,1,128]{3,1,2,0:T(8,128)(2,1)S(1)} %get-tuple-element.565, s32[]{:T(128)} %get-tuple-element.542, f32[896]{0:T(1024)S(1)} %get-tuple-element.526, ...), kind=kOutput, calls=%fused_computation.12.clone.1 | convolution fusion | flops 245317632 | bytes 4882438 | tf_op jit(solution)/shard_map/cond/branch_1_fun/while/body/eval_jaxpr/gqk,kgd->gqd/dot_general | solution.py:91
  317.7 2.5 fusion.60
  320.2 1.3 fusion.61
  321.5 0.7 reduce.12
  322.2 1.2 divide_convert_fusion
  323.6 0.8 copy.31
  (75 shorter events, 1.6 us)
Async XLA Ops:
  6.5 106.3 %all-gather.4.cloned.1.call-start = ((), (), s32[]{:S(2)}) async-start(), calls=%async_computation.1 | async-start | bytes 16773120 | tf_op jit(solution)/shard_map/all_gather | solution.py:48
  9.4 16.8 %all-to-all-start = ((bf16[4,128,896]{1,2,0:T(8,128)(2,1)}), bf16[4,128,896]{1,2,0:T(8,128)(2,1)S(1)}, u32[]{:S(2)}, u32[]{:S(2)}) async-start(bf16[4,128,896]{1,2,0:T(8,128)(2,1)} %broadcast_in_dim.40), calls=%async_computation | async-start | bytes 1835008 | tf_op jit(solution)/shard_map/all_to_all | solution.py:25
  14.3 183.9 %all-gather.6.cloned.1.call-start = ((), (), s32[]{:S(2)}) async-start(), calls=%async_computation.2 | async-start | bytes 4259840 | tf_op jit(solution)/shard_map/all_gather | solution.py:40
  112.8 10.3 %copy-start.1 = (s32[128]{0:T(128)S(1)}, s32[128]{0:T(128)}, u32[]{:S(2)}) copy-start(s32[128]{0:T(128)} %param.10) | copy-start | bytes 1540
  207.8 5.5 %copy-start = (f32[1024,896]{1,0:T(8,128)S(1)}, f32[1024,896]{1,0:T(8,128)}, u32[]{:S(2)}) copy-start(f32[1024,896]{1,0:T(8,128)} %get-tuple-element.524) | copy-start | bytes 11010052 | tf_op jit(solution)/shard_map/cond/branch_1_fun/while
  222.1 5.6 %copy-start = (f32[1024,896]{1,0:T(8,128)S(1)}, f32[1024,896]{1,0:T(8,128)}, u32[]{:S(2)}) copy-start(f32[1024,896]{1,0:T(8,128)} %get-tuple-element.524) | copy-start | bytes 11010052 | tf_op jit(solution)/shard_map/cond/branch_1_fun/while
  237.1 5.6 %copy-start = (f32[1024,896]{1,0:T(8,128)S(1)}, f32[1024,896]{1,0:T(8,128)}, u32[]{:S(2)}) copy-start(f32[1024,896]{1,0:T(8,128)} %get-tuple-element.524) | copy-start | bytes 11010052 | tf_op jit(solution)/shard_map/cond/branch_1_fun/while
  252.1 5.6 %copy-start = (f32[1024,896]{1,0:T(8,128)S(1)}, f32[1024,896]{1,0:T(8,128)}, u32[]{:S(2)}) copy-start(f32[1024,896]{1,0:T(8,128)} %get-tuple-element.524) | copy-start | bytes 11010052 | tf_op jit(solution)/shard_map/cond/branch_1_fun/while
  267.1 5.6 %copy-start = (f32[1024,896]{1,0:T(8,128)S(1)}, f32[1024,896]{1,0:T(8,128)}, u32[]{:S(2)}) copy-start(f32[1024,896]{1,0:T(8,128)} %get-tuple-element.524) | copy-start | bytes 11010052 | tf_op jit(solution)/shard_map/cond/branch_1_fun/while
  282.1 5.6 %copy-start = (f32[1024,896]{1,0:T(8,128)S(1)}, f32[1024,896]{1,0:T(8,128)}, u32[]{:S(2)}) copy-start(f32[1024,896]{1,0:T(8,128)} %get-tuple-element.524) | copy-start | bytes 11010052 | tf_op jit(solution)/shard_map/cond/branch_1_fun/while
  297.1 5.6 %copy-start = (f32[1024,896]{1,0:T(8,128)S(1)}, f32[1024,896]{1,0:T(8,128)}, u32[]{:S(2)}) copy-start(f32[1024,896]{1,0:T(8,128)} %get-tuple-element.524) | copy-start | bytes 11010052 | tf_op jit(solution)/shard_map/cond/branch_1_fun/while
  312.2 5.6 %copy-start = (f32[1024,896]{1,0:T(8,128)S(1)}, f32[1024,896]{1,0:T(8,128)}, u32[]{:S(2)}) copy-start(f32[1024,896]{1,0:T(8,128)} %get-tuple-element.524) | copy-start | bytes 11010052 | tf_op jit(solution)/shard_map/cond/branch_1_fun/while
Sparse Core Ops, SparseCore 0:
  10.0 102.7 all-gather.3
  122.1 76.0 all-gather.5
where the time goes:
time: 332 us; the launch traced here: 331 us
  waiting for transfers between devices  135 us (41%)
  matrix products  88 us (27%)
  blocking collectives  38.5 us (12%)
  other arithmetic  37.5 us (11%)
  between operations  14.7 us (4%)
  local copies, waits for them, and re-layouts  12.3 us (4%)
  starting transfers between devices  4.83 us (1%)
    all_gather x1, waiting for transfers between devices, local(): shard_piece = lax.all_gather(w_proj, 'seq', axis=1, tiled=True)  86.6 us
    dot_general x8, matrix products, absorb(): jnp.einsum('gqk,kgd->gqd', weights.astype(jnp.bfloat16), value_part, pref...  44.4 us
    all_gather x1, blocking collectives, local(): lax.all_gather(segment, 'seq', axis=0, tiled=True)  38.5 us
    all_gather x1, waiting for transfers between devices, sent_together(): lax.all_gather(both, axis, axis=dim, tiled=True)  36.3 us
    dot_general x8, matrix products, absorb(): jnp.einsum('gqd,kgd->gqk', query_lay, key_part, preferred_element_type=jn...  35.5 us
    reduce_sum x8, other arithmetic, absorb(): running_sum = running_sum * shrink + jnp.sum(weights, axis=2)  19.8 us
    all_to_all x1, waiting for transfers between devices, copy_for_each(): lax.all_to_all(jnp.broadcast_to(array[None], (peers, *array.shape)), axis...  11.3 us
    add x8, other arithmetic, absorb(): running_sum = running_sum * shrink + jnp.sum(weights, axis=2)  9.64 us
  transfers between devices with their start and end apart: 3, of which 3 were waited for; matrix products, arithmetic and copies ran while one was open for 1% of the time, Pallas kernels for 0%

commit v1 on v0

v1 whole, which is shorter than its diff:
```python
import math

import jax
import jax.numpy as jnp
from jax import lax
from jax.experimental import pallas as pl
from jax.experimental.pallas import tpu as pltpu
from jax.sharding import PartitionSpec as P

HEADS = 7
D = 128
BLOCK = 128
WINDOW = 33
CHUNKS = 3
PER = WINDOW // CHUNKS
FAR = -1e30
SCALE = math.log2(math.e) / math.sqrt(D)
MESH = pl.DeviceIdType.MESH
DEPTH = 3584
PART = DEPTH // 4
SLAB = 56
PLANE = 8 * SLAB
ROWS = 144
COPIES = 200


def project(tok, w, meta, proj, kv, T, W, mb, acc, ob, vb, vp, send, recv, near):
    s, x = lax.axis_index("seq"), lax.axis_index("tp")
    z, y, c = s // 8, (s // 2) % 4, s % 2

    def at(dz=0, dy=0, dc=0, dx=0):
        return (((z + dz) % 8) * 8 + ((y + dy) % 4) * 2 + (c + dc) % 2, (x + dx) % 4)

    made = []

    def remote(src, dst, device):
        k = len(made)
        made.append(
            pltpu.make_async_remote_copy(
                src_ref=src,
                dst_ref=dst,
                send_sem=send.at[k],
                recv_sem=recv.at[k],
                device_id=device,
                device_id_type=MESH,
            )
        )
        return made[-1]

    def go(src, dst, device):
        copy = remote(src, dst, device)
        copy.start()
        return copy

    barrier = pltpu.get_barrier_semaphore()
    peers = [at(dx=1), at(dx=3), at(dz=1), at(dz=7)]
    peers += [at(dy=d, dc=e) for d in range(4) for e in range(2) if d or e]
    for peer in peers:
        pl.semaphore_signal(barrier, inc=1, device_id=peer, device_id_type=MESH)
    pl.semaphore_wait(barrier, len(peers))

    def cols(j):
        return pl.ds(pl.multiple_of((j % 4) * PART, 128), PART)

    def rows_of(plane):
        return pl.ds(pl.multiple_of(((plane + 8) % 8) * PLANE, 64), PLANE)

    def head_cols(j):
        return pl.ds(pl.multiple_of(j * D, 128), D)

    mine = pl.ds(pl.multiple_of(s * SLAB, 8), SLAB)
    spread = z // 2

    local = []
    first, ninth = [], []
    for d in range(4):
        for e in range(2):
            there, m = (y + d) % 4, (c + e) % 2
            for h in range(2):
                src, dst = w.at[m, :, head_cols(2 * there + h)], W.at[m, h, mine, :]
                if d or e:
                    first.append(go(src, dst, at(dy=d, dc=e)))
                else:
                    local.append(pltpu.make_async_copy(src, dst, near.at[h]))
                    local[-1].start()
            src, dst = w.at[m, :, pl.ds(8 * D, D)], W.at[m, 2, mine, :]
            if d or e:
                copy = remote(src, dst, at(dy=d, dc=e))
                ninth.append((d, copy))
                pl.when(there == spread)(copy.start)
            else:
                own = pltpu.make_async_copy(src, dst, near.at[2])
                pl.when(y == spread)(own.start)
    metas = [
        go(meta, mb.at[y * 2 + c], at(dy=d, dc=e)) for d in range(4) for e in range(2) if d or e
    ]
    for src, dst, k in (
        (tok, T.at[y, :, cols(x)], 3),
        (meta, mb.at[y * 2 + c], 4),
    ):
        local.append(pltpu.make_async_copy(src, dst, near.at[k]))
        local[-1].start()

    class Ring:
        def __init__(self, axis, piece, src=None):
            self.axis, self.piece = axis, piece
            self.me = y if axis == "dy" else x
            own = piece(self.me % 4, None) if src is None else src
            self.a = go(own, piece(self.me % 4, None), at(**{axis: 1}))
            self.b = go(own, piece(self.me % 4, None), at(**{axis: 3}))

        def forward(self):
            self.a.wait_recv()
            part = self.piece((self.me + 3) % 4, 0)
            self.f = go(part, part, at(**{self.axis: 1}))
            self.b.wait_recv()
            part = self.piece((self.me + 1) % 4, 1)
            self.g = go(part, part, at(**{self.axis: 3}))

        def finish(self):
            self.f.wait_recv()
            self.g.wait_recv()

    def top_piece(row, j, half):
        r = pl.ds(0, 64) if half is None else pl.ds(32 * half, 32)
        return T.at[row % 4, r, cols(j)]

    def low_piece(row, j, half):
        r = pl.ds(64, 64) if half is None else pl.ds(64 + 32 * half, 32)
        return T.at[row % 4, r, cols(j)]

    top, low = tok.at[pl.ds(0, 64), :], tok.at[pl.ds(64, 64), :]
    top_y = Ring("dy", lambda j, h: top_piece(j, x, h), top)
    low_x = Ring("dx", lambda j, h: low_piece(y, j, h), low)
    top_x = [Ring("dx", lambda j, h: top_piece(y, j, h), top)]
    low_y = [Ring("dy", lambda j, h: low_piece(j, x, h), low)]

    def top_more(d):
        top_x.append(Ring("dx", lambda j, h: top_piece(y + d, j, h)))

    def low_more(d):
        low_y.append(Ring("dy", lambda j, h: low_piece(j, x + d, h)))

    for copy in first:
        copy.wait_recv()
    for copy in local[:2]:
        copy.wait()

    @pl.when(y == spread)
    def _():
        for _, copy in ninth:
            copy.wait_recv()
        own.wait()

    def third(o):
        return ((o + 8) % 8) // 2 == y

    ring, side, special, special_side = {}, [], {}, []

    def share(h, o, rows=None):
        ref = W.at[c, h, rows_of(o) if rows is None else rows, :]
        side.append(go(ref, ref, at(dc=1)))

    def half_rows(o, half):
        return pl.ds(pl.multiple_of(((o + 8) % 8) * PLANE + half * (PLANE // 2), 32), PLANE // 2)

    def launch(t):
        for way, sign in ((0, 1), (1, -1)):
            o = z - sign * t
            for h in range(2) if t < 3 else (way,):
                ref = W.at[c, h, rows_of(o), :]
                ring[way, t, h] = go(ref, ref, at(dz=1 if way == 0 else 7))
            r = rows_of(o) if t < 3 else half_rows(o, way)
            ref = W.at[c, 2, r, :]
            copy = special[way, t] = remote(ref, ref, at(dz=1 if way == 0 else 7))
            pl.when(third(o))(copy.start)

    def extra_side(o, rows=None):
        ref = W.at[c, 2, rows_of(o) if rows is None else rows, :]
        copy = remote(ref, ref, at(dc=1))
        special_side.append((o, copy))
        pl.when(third(o))(copy.start)

    def arrive(t):
        for way, sign in ((0, 1), (1, -1)):
            o = z - sign * (t + 1)
            for h in range(2) if t < 3 else (way,):
                ring[way, t, h].wait_recv()
            pl.when(third(o))(special[way, t].wait_recv)

    def pass_on(t):
        for way, sign in ((0, 1), (1, -1)):
            o = z - sign * (t + 1)
            for h in range(2) if t < 3 else (way,):
                share(h, o)
            extra_side(o, None if t < 3 else half_rows(o, way))

    launch(0)
    for h in range(2):
        share(h, z)
    extra_side(z)

    top_y.forward()
    low_x.forward()
    for d in (3, 1):
        top_more(d)
        low_more(d)
    top_x[0].forward()
    low_y[0].forward()
    top_y.finish()
    low_x.finish()
    top_more(2)
    low_more(2)
    arrive(0)
    launch(1)
    pass_on(0)
    for k in (1, 2):
        top_x[k].forward()
        low_y[k].forward()
    arrive(1)
    launch(2)
    pass_on(1)
    top_x[3].forward()
    low_y[3].forward()
    arrive(2)
    launch(3)
    pass_on(2)
    for k in range(4):
        top_x[k].finish()
        low_y[k].finish()
    for copy in metas:
        copy.wait_recv()
    for copy in local[2:]:
        copy.wait()
    arrive(3)
    pass_on(3)
    for copy in side:
        copy.wait_recv()
    for o, copy in special_side:
        pl.when(third(o))(copy.wait_recv)

    def multiply(k, unused):
        at_cols = pl.ds(pl.multiple_of(k * PART, 128), PART)
        lhs = T[:, :, at_cols].reshape(4 * BLOCK, PART)
        rhs = jnp.concatenate([W[m, h, at_cols, :] for m in range(2) for h in range(2)], axis=1)
        acc[...] += jnp.dot(lhs, rhs, preferred_element_type=jnp.float32)
        return unused

    acc[...] = jnp.zeros_like(acc)
    lax.fori_loop(0, 4, multiply, 0)
    lhs = T[:, :, cols(y)].reshape(4 * BLOCK, PART)
    rhs = jnp.concatenate([W[m, 2, cols(y), :] for m in range(2)], axis=1)
    last = jnp.dot(lhs, rhs, preferred_element_type=jnp.float32)
    for j in range(4):
        generated = mb[j * 2 + c, 1:2, :] == 1.0
        r = slice(j * BLOCK, (j + 1) * BLOCK)
        for h in range(2):
            ob[j, :, h * D : (h + 1) * D] = jnp.where(
                generated, acc[r, (2 + h) * D : (3 + h) * D], acc[r, h * D : (h + 1) * D]
            ).astype(jnp.bfloat16)
        vb[j] = jnp.where(generated, last[r, D:], last[r, :D])
    out = []
    for d in (1, 3, 2):
        there = (y + d) % 4
        out.append(go(vb.at[there], vp.at[y], at(dy=d)))
        out.append(go(ob.at[there], proj.at[y], at(dy=d)))
    proj[y] = ob[y]
    vp[y] = vb[y]
    for copy in out:
        copy.wait_recv()

    here = y * 2 + c
    kv[4, here, :BLOCK, :D] = proj[3, :, D:]
    kv[4, here, :BLOCK, D:] = (vp[0] + vp[1] + vp[2] + vp[3]).astype(jnp.bfloat16)
    kv[4, here, BLOCK:, :D] = jnp.broadcast_to(meta[0:1, :], (ROWS - BLOCK, D)).astype(jnp.bfloat16)
    kv[4, here, BLOCK:, D:] = jnp.zeros((ROWS - BLOCK, D), jnp.bfloat16)

    def kv_piece(p, j, half):
        r = pl.ds(0, ROWS) if half is None else (pl.ds(0, 64), pl.ds(64, ROWS - 64))[half]
        return kv.at[p, (j % 4) * 2 + c, r, :]

    def to_side(p, j):
        ref = kv_piece(p, j, None)
        out.append(go(ref, ref, at(dc=1)))
        return out[-1]

    back, around, crossed = [], [], []
    for t in range(5):
        p = 4 - t
        if t:
            back[-1].wait_recv()
        if t < 4:
            back.append(go(kv.at[p, here], kv.at[p - 1, here], at(dz=1)))
        around.append(Ring("dy", lambda j, h, p=p: kv_piece(p, j, h)))
        crossed.append(to_side(p, y))
        if t:
            around[t - 1].forward()
            crossed += [to_side(p + 1, y + 3), to_side(p + 1, y + 1)]
    around[4].forward()
    crossed += [to_side(0, y + 3), to_side(0, y + 1)]
    for t in range(5):
        around[t].finish()
        crossed.append(to_side(4 - t, y + 2))
    for copy in crossed:
        copy.wait_recv()

    conditional = {id(copy) for _, copy in ninth} | {id(copy) for copy in special.values()}
    conditional |= {id(copy) for _, copy in special_side}
    for copy in made:
        if id(copy) not in conditional:
            copy.wait_send()
    for d, copy in ninth:
        pl.when((y + d) % 4 == spread)(copy.wait_send)
    for (way, t), copy in special.items():
        pl.when(third(z - t if way == 0 else z + t))(copy.wait_send)
    for o, copy in special_side:
        pl.when(third(o))(copy.wait_send)


def gather_and_project(tokens, weights, meta):
    vmem = pl.BlockSpec(memory_space=pltpu.VMEM)
    return pl.pallas_call(
        project,
        name="project",
        out_shape=(
            jax.ShapeDtypeStruct((4, BLOCK, 2 * D), jnp.bfloat16),
            jax.ShapeDtypeStruct((5, 8, ROWS, 2 * D), jnp.bfloat16),
        ),
        in_specs=[vmem] * 3,
        out_specs=(vmem, vmem),
        scratch_shapes=[
            pltpu.VMEM((4, BLOCK, DEPTH), jnp.bfloat16),
            pltpu.VMEM((2, 3, DEPTH, D), jnp.bfloat16),
            pltpu.VMEM((8, 8, D), jnp.float32),
            pltpu.VMEM((4 * BLOCK, 4 * D), jnp.float32),
            pltpu.VMEM((4, BLOCK, 2 * D), jnp.bfloat16),
            pltpu.VMEM((4, BLOCK, D), jnp.float32),
            pltpu.VMEM((4, BLOCK, D), jnp.float32),
            pltpu.SemaphoreType.DMA((COPIES,)),
            pltpu.SemaphoreType.DMA((COPIES,)),
            pltpu.SemaphoreType.DMA((5,)),
        ],
        compiler_params=pltpu.CompilerParams(
            collective_id=0, has_side_effects=True, vmem_limit_bytes=40 << 20
        ),
    )(tokens, weights, meta)


def attend(place, proj, kv, o_ref, qa, ka, va, acc, top, seg):
    eye = (
        lax.broadcasted_iota(jnp.int32, (BLOCK, D), 0)
        == lax.broadcasted_iota(jnp.int32, (BLOCK, D), 1)
    ).astype(jnp.bfloat16)
    for h in range(HEADS):
        qa[h * BLOCK : (h + 1) * BLOCK, :D] = proj[h // 2, :, (h % 2) * D : (h % 2 + 1) * D]
        qa[h * BLOCK : (h + 1) * BLOCK, D:] = eye
    va[:, D:] = jnp.ones((WINDOW * BLOCK, D), jnp.bfloat16)
    first = place[1]
    missing = 32 - place[2]
    for j in range(WINDOW):
        row = kv[first + j, BLOCK:, :D][0:1].astype(jnp.float32)
        seg[j : j + 1, :] = jnp.where(j < missing, -1.0, row)
    seg_row = seg[WINDOW - 1 : WINDOW, :]
    seg_cols = seg[...].T
    key = lax.broadcasted_iota(jnp.int32, (BLOCK, BLOCK), 0)
    query = lax.broadcasted_iota(jnp.int32, (BLOCK, BLOCK), 1)
    reach = jnp.where(place[0] == 1, BLOCK, query)
    for j in range(WINDOW):
        rows = slice(j * BLOCK, (j + 1) * BLOCK)
        ka[rows, :D] = kv[first + j, :BLOCK, :D]
        va[rows, :D] = kv[first + j, :BLOCK, D:]
        same = seg_cols[:, j : j + 1] == seg_row
        if j == WINDOW - 1:
            same = same & (key <= reach)
        ka[rows, D:] = jnp.where(same, 0.0, FAR).astype(jnp.bfloat16)

    top[...] = jnp.full_like(top, -3e38)
    acc[...] = jnp.zeros_like(acc)

    def step(i, unused):
        c = CHUNKS - 1 - i
        rows = pl.ds(pl.multiple_of(c * (PER * BLOCK), BLOCK), PER * BLOCK)
        s = lax.dot_general(
            qa[...], ka[rows, :], (((1,), (1,)), ((), ())), preferred_element_type=jnp.float32
        )
        old = top[...]
        new = jnp.maximum(old, jnp.max(s, axis=1, keepdims=True))
        top[...] = new
        p = jnp.exp2((s - new) * SCALE).astype(jnp.bfloat16)
        shrink = jnp.exp2((old - new) * SCALE)
        acc[...] = acc[...] * shrink + jnp.dot(p, va[rows, :], preferred_element_type=jnp.float32)
        return unused

    lax.fori_loop(0, CHUNKS, step, 0)
    for h in range(HEADS):
        part = acc[h * BLOCK : (h + 1) * BLOCK, :]
        o_ref[:, h * D : (h + 1) * D] = (part[:, :D] / part[:, D:]).astype(jnp.bfloat16)


def attention(place, proj, kv):
    vmem = pl.BlockSpec(memory_space=pltpu.VMEM)
    return pl.pallas_call(
        attend,
        name="attend",
        out_shape=jax.ShapeDtypeStruct((BLOCK, HEADS * D), jnp.bfloat16),
        in_specs=[pl.BlockSpec(memory_space=pltpu.SMEM), vmem, vmem],
        out_specs=vmem,
        scratch_shapes=[
            pltpu.VMEM((HEADS * BLOCK, 2 * D), jnp.bfloat16),
            pltpu.VMEM((WINDOW * BLOCK, 2 * D), jnp.bfloat16),
            pltpu.VMEM((WINDOW * BLOCK, 2 * D), jnp.bfloat16),
            pltpu.VMEM((HEADS * BLOCK, 2 * D), jnp.float32),
            pltpu.VMEM((HEADS * BLOCK, 1), jnp.float32),
            pltpu.VMEM((40, BLOCK), jnp.float32),
        ],
        compiler_params=pltpu.CompilerParams(vmem_limit_bytes=48 << 20),
    )(place, proj, kv.reshape(40, ROWS, 2 * D))


def local(tokens, modality, segment, w_proj):
    here = lax.axis_index("seq")
    meta = jnp.concatenate(
        [
            segment.astype(jnp.float32)[None],
            jnp.broadcast_to(modality.astype(jnp.float32)[:, None], (1, BLOCK)),
            jnp.zeros((6, BLOCK), jnp.float32),
        ]
    )
    proj, kv = gather_and_project(tokens, w_proj, meta)
    place = jnp.stack([modality[0], here % 8, here])
    return attention(place, proj, kv)


def solution(mesh):
    return jax.shard_map(
        local,
        mesh=mesh,
        in_specs=(P("seq", "tp"), P("seq"), P("seq"), P(None, "seq", "tp")),
        out_specs=P("seq", "tp"),
        check_vma=False,
    )
```

time: 332 us -> 105 us (0.32)
  waiting for transfers between devices: 135 us -> 0 us
  Pallas kernels: 0 us -> 102 us
  matrix products: 88 us -> 0 us
  blocking collectives: 38.5 us -> 0 us
  other arithmetic: 37.5 us -> 0.81 us
  between operations: 14.7 us -> 0.67 us
  local copies, waits for them, and re-layouts: 12.3 us -> 2.04 us
  starting transfers between devices: 4.83 us -> 0 us
    all_gather x2 -> x0, waiting for transfers between devices: 123 us -> none  [the longest x1 86.6 us: local(): shard_piece = lax.all_gather(w_proj, 'seq', axis=1, tiled=True)]
    pallas_call x0 -> x2, Pallas kernels: none -> 102 us  [the longest x1 87 us: gather_and_project(): pl.pallas_call(project, name='project', out_shape=(jax.ShapeDtypeStruct((...]
    dot_general x17 -> x0, matrix products: 88 us -> none  [the longest x8 44.4 us: absorb(): jnp.einsum('gqk,kgd->gqd', weights.astype(jnp.bfloat16), value_part, pref...]
    all_gather x1 -> x0, blocking collectives: 38.5 us -> none  [local(): lax.all_gather(segment, 'seq', axis=0, tiled=True)]
    reduce_sum x8 -> x0, other arithmetic: 19.8 us -> none  [absorb(): running_sum = running_sum * shrink + jnp.sum(weights, axis=2)]
    all_to_all x1 -> x0, waiting for transfers between devices: 11.3 us -> none  [copy_for_each(): lax.all_to_all(jnp.broadcast_to(array[None], (peers, *array.shape)), axis...]
    add x8 -> x0, other arithmetic: 9.64 us -> none  [absorb(): running_sum = running_sum * shrink + jnp.sum(weights, axis=2)]
    all_to_all x1 -> x0, starting transfers between devices: 4.83 us -> none  [copy_for_each(): lax.all_to_all(jnp.broadcast_to(array[None], (peers, *array.shape)), axis...]
  transfers between devices with their start and end apart: 3 -> 0, of which waited for: 3 -> 0; matrix products, arithmetic and copies ran while one was open for 1% -> 0% of each run, Pallas kernels for 0% -> 0%
where the time goes in v1:
time: 105 us
  Pallas kernels  102 us (97%)
  local copies, waits for them, and re-layouts  2.04 us (2%)
    pallas_call x1, Pallas kernels, gather_and_project(): pl.pallas_call(project, name='project', out_shape=(jax.ShapeDtypeStruct((...  87 us
    pallas_call x1, Pallas kernels, attention(): pl.pallas_call(attend, name='attend', out_shape=jax.ShapeDtypeStruct((BLO...  14.7 us

profile of v1, /device:TPU:1, one launch (start us, length us, event | category | flops | bytes accessed | tf_op | source)
XLA Modules:
  0.0 105.2 jit_solution(12990153548184384054)
XLA Ops:
  0.7 0.1 pad_add_fusion.place
  0.7 0.1 pad.1.clone
  0.8 0.7 convert_bitcast_fusion
  1.5 0.1 pad.2.clone
  1.5 0.1 maximum_maximum_fusion.meta
  1.6 0.0 copy-start
  1.6 0.9 copy-done
  2.6 0.0 copy-start.1
  2.6 0.9 copy-done.1
  3.5 87.0 %project.1 = (bf16[4,128,256]{2,1,0:T(8,128)(2,1)S(1)}, bf16[5,8,144,256]{3,2,1,0:T(8,128)(2,1)S(1)}) custom-call(bf16[128,896]{1,0:T(8,128)(2,1)S(1)} %copy-done.1, bf16[2,56,1152]{2,1,0:T(8,128)(2,1)S(1)} %copy-done, f32[8,128]{1,0:T(8,128)S(1)} %maximum_maximum_fusion.meta), custom_call_target="tpu_custom_call" | custom-call | tf_op jit(solution)/shard_map/project/pallas_call | solution.py:322
  90.5 14.7 %attend.1 = bf16[128,896]{1,0:T(8,128)(2,1)} custom-call(s32[3]{0:T(128)S(1)} %pad_add_fusion.place, bf16[4,128,256]{2,1,0:T(8,128)(2,1)S(1)} %get-tuple-element.7.proj, bf16[40,144,256]{2,1,0:T(8,128)(2,1)S(1)} %bitcast.6), custom_call_target="tpu_custom_call" | custom-call | tf_op jit(solution)/shard_map/attend/pallas_call | solution.py:402
  (1 shorter events, 0.0 us)
Async XLA Ops:
  1.6 0.9 copy-start
  2.6 0.9 copy-start.1
